TPU v7x, 128 devices: a whole 4x4x4 slice. The times are simulated.
128 devices in a mesh: sector: 8 (over x_hi, z), group: 16 (over y, x_lo, core).
Axes of the slice: x: 4 (x_hi: 2, x_lo: 2; x = x_hi * 2 + x_lo), y: 4, z: 4, core: 2. Of those that a mesh axis runs over, the one named last changes fastest.
Arguments:
- spectrum: float32 [1152, 128, 1024], P('group', None, 'sector'), may hold values from 0.1 to 2
- land_mask: int32 [128, 1024], P(None, 'sector'), may hold values 0 or 1
- wind_field: float32 [2, 128, 1024], P(None, 'group', 'sector'), may hold values from -3 to 3
- assignment: int32 [1152], replicated, may hold values from 0 to 1151, each once
- courant: float32 [32], replicated, may hold values from 0.3 to 0.65
- growth: float32 [32], replicated, may hold values from 0.1 to 0.5
- whitecap: float32 [32], replicated, may hold values from 0.2 to 1
- weights: float32 [32], replicated, may hold values from 0.5 to 5
- spread: float32 [32, 36, 36], replicated, may hold values from -1 to 1
Outputs:
- updated: float32 [1152, 128, 1024], P('group', None, 'sector')
Inputs may be any that keep to these rules, and one draw needn't show every extreme that they name: `assignment`: each component number appears exactly once.
All inputs are finite; a program needn't handle non-finite values. No bound on the sum of `land_mask` on one device may be relied on, other than what follows from the above.
Results may differ from a plain program's by a relative error of at most 0.00007.
Values sent between devices are 32-bit elements; how exact they have to be, the bound alone decides.
A program may use at most 128 MiB of HBM per device.

v0:
```python
import functools
import math

import jax
import jax.numpy as jnp
import numpy as np
from jax import lax
from jax.experimental import pallas as pl
from jax.experimental.pallas import tpu as pltpu
from jax.sharding import PartitionSpec as P

MESH = pl.DeviceIdType.MESH
DIRS = 36
FREQ = 32
SUBSTEPS = 6
LAT = 128
LANES = 128
EDGE = SUBSTEPS
SLOT = 2 * EDGE
SUB = 8
EARLY = 6
F32 = jnp.float32
BF16 = jnp.bfloat16


def relu(x):
    return jnp.maximum(x, 0.0)


def kernel(n, ns, comps, spec, icos, lm, wind, cprm, sprm, fprm, rmeta, sphl, out,
           x, p, r, acc, cph, cpl, outs, own, te, tw, ter, twr, s, sm, mb, ld, w16,
           load_sem, halo_send, halo_recv, send1, recv1, send2, recv2):
    me = lax.axis_index("group")
    sec = lax.axis_index("sector")
    east, west = lax.rem(sec + 1, ns), lax.rem(sec + ns - 1, ns)
    total = n * comps
    groups = comps // SUB
    block = LAT // n
    span = n * SUB

    def load(g):
        rows = pl.ds(g * SUB * LAT, SUB * LAT)
        return pltpu.make_async_copy(spec.at[rows], x.at[rows], load_sem.at[g])

    for g in range(groups):
        load(g).start()

    barrier = pltpu.get_barrier_semaphore()

    @pl.loop(1, n)
    def _(k):
        pl.semaphore_signal(barrier, inc=1, device_id={"group": lax.rem(me + k, n)}, device_id_type=MESH)

    for side in (east, west):
        pl.semaphore_signal(barrier, inc=1, device_id={"sector": side}, device_id_type=MESH)

    lane = lax.broadcasted_iota(jnp.int32, (SUB, LANES), 1)
    first = lax.rem(lane, SLOT) < EDGE

    @pl.loop(0, LAT // SUB)
    def _(t):
        for i in range(SUB):
            j = t * SUB + i
            mb[j] = jnp.broadcast_to(lm[pl.ds(j, 1), :].astype(F32), (SUB, LANES))

    for g in range(groups):
        load(g).wait()

    @pl.loop(0, LAT // 4)
    def _(t):
        for i in range(4):
            j = t * 4 + i
            packed = pltpu.roll(mb[j], EDGE + SLOT * groups, axis=1)
            for g in range(groups):
                tile = x[pl.ds(g * SUB * LAT + j, SUB, stride=LAT), :]
                tile = pltpu.roll(tile, EDGE + SLOT * g, axis=1)
                packed = jnp.where((lane >= SLOT * g) & (lane < SLOT * (g + 1)), tile, packed)
            own[j] = packed

    half = LAT // 2

    @pl.loop(0, half // 4)
    def _(t):
        for i in range(4):
            j = t * 4 + i
            low, high = own[j], own[j + half]
            te[j] = jnp.where(first, low, pltpu.roll(high, EDGE, axis=1))
            tw[j] = jnp.where(first, pltpu.roll(high, LANES - EDGE, axis=1), low)

    pl.semaphore_wait(barrier, n + 1)

    def halo(src, dst, k, side):
        return pltpu.make_async_remote_copy(
            src_ref=src, dst_ref=dst, send_sem=halo_send.at[k], recv_sem=halo_recv.at[k],
            device_id={"sector": side}, device_id_type=MESH)

    to_east = halo(te, ter, 0, east)
    to_west = halo(tw, twr, 1, west)
    to_east.start()
    to_west.start()

    def sweep(read, write, mask, coefs):
        rate, keep, north, sx, sy = coefs

        def rows(j0, prev, cur, nexts):
            tiles = [prev, cur] + nexts
            for i in range(SUB):
                e = tiles[i + 1]
                fx = jnp.where(sx, pltpu.roll(e, 1, axis=1), pltpu.roll(e, LANES - 1, axis=1))
                fy = jnp.where(sy, tiles[i], tiles[i + 2])
                new = keep * e + north * fy + (rate * icos[j0 + i]) * (fx - e)
                write(j0 + i, new * mask(j0 + i))
            return tiles[SUB], tiles[SUB + 1]

        def body(t, carry):
            j0 = t * SUB
            return rows(j0, *carry, [read(j0 + 1 + i) for i in range(SUB)])

        zero = jnp.zeros((SUB, LANES), F32)
        prev, cur = lax.fori_loop(0, LAT // SUB - 1, body, (zero, read(0)))
        j0 = LAT - SUB
        rows(j0, prev, cur, [read(j0 + 1 + i) for i in range(SUB - 1)] + [zero])

    def spread_columns(ref, start, count):
        tile = ref[pl.ds(start, SUB), :]
        return [jnp.broadcast_to(tile[:, k:k + 1], (SUB, LANES)) for k in range(count)]

    def mask_row(j):
        return mb[j]

    def main(g):
        rate, keep, north, sx, sy = spread_columns(cprm, pl.multiple_of(g * SUB, SUB), 5)
        coefs = (rate, keep, north, sx > 0.0, sy > 0.0)
        mine = pl.ds(pl.multiple_of(g * SUB, SUB), SUB)

        def write(j, v):
            p[j, mine, :] = v

        sweep(lambda j: x[pl.ds(g * SUB * LAT + j, SUB, stride=LAT), :], write, mask_row, coefs)

        @pl.loop(1, SUBSTEPS)
        def _(_k):
            sweep(lambda j: p[j, mine, :], write, mask_row, coefs)

    def shuffle(g, k):
        peer = lax.rem(me + k, n)
        return pltpu.make_async_remote_copy(
            src_ref=p.at[pl.ds(pl.multiple_of(peer * block, block), block), pl.ds(pl.multiple_of(g * SUB, SUB), SUB), :],
            dst_ref=r.at[:, pl.ds(pl.multiple_of(g * span + me * SUB, SUB), SUB), :],
            send_sem=send1.at[g * n + k], recv_sem=recv1.at[g * n + k],
            device_id={"group": peer}, device_id_type=MESH)

    def keep_mine(g):
        return pltpu.make_async_copy(
            p.at[pl.ds(pl.multiple_of(me * block, block), block), pl.ds(pl.multiple_of(g * SUB, SUB), SUB), :],
            r.at[:, pl.ds(pl.multiple_of(g * span + me * SUB, SUB), SUB), :],
            recv1.at[g * n])

    def merge(g):
        (sx,) = spread_columns(cprm, pl.multiple_of(g * SUB, SUB), 4)[3:]
        seam = jnp.where(sx > 0.0, (lane < EDGE).astype(F32), (lane >= LANES - EDGE).astype(F32)) > 0.0
        mine = pl.ds(pl.multiple_of(g * SUB, SUB), SUB)
        shift = LANES - EDGE - SLOT * g

        @pl.loop(0, LAT // SUB)
        def _(t):
            for i in range(SUB):
                j = t * SUB + i
                p[j, mine, :] = jnp.where(seam, pltpu.roll(s[j], shift, axis=1), p[j, mine, :])

        @pl.loop(1, n)
        def _(k):
            shuffle(g, k).start()

        keep_mine(g).start()

    @pl.loop(0, EARLY)
    def _(g):
        main(g)

    to_east.wait_recv()
    to_west.wait_recv()
    scoefs = [sprm[pl.ds(k * SUB, SUB), :] for k in range(5)]
    eastward = scoefs[3] > 0.0
    lastslot = (lane >= SLOT * groups) & (lane < SLOT * (groups + 1))

    def fan(v):
        v1 = jnp.where(lastslot, v, 0.0)
        v2 = v1 + pltpu.roll(v1, LANES - SLOT, axis=1)
        v4 = v2 + pltpu.roll(v2, LANES - 2 * SLOT, axis=1)
        v8 = v4 + pltpu.roll(v4, LANES - 4 * SLOT, axis=1)
        return v8 + pltpu.roll(v2, LANES - 8 * SLOT, axis=1)

    @pl.loop(0, half // 2)
    def _(t):
        for i in range(2):
            j = t * 2 + i
            fe, fw = ter[j], twr[j]
            for row, ve, vw in ((j, fe, fw), (j + half, pltpu.roll(fe, LANES - EDGE, axis=1), pltpu.roll(fw, EDGE, axis=1))):
                o = own[row]
                xe = jnp.where(first, ve, o)
                xw = jnp.where(first, o, vw)
                s[row] = jnp.where(eastward, xe, xw)
                sm[row] = jnp.where(eastward, fan(xe), fan(xw))

    def write_strip(j, v):
        s[j] = v

    @pl.loop(0, SUBSTEPS)
    def _(_k):
        sweep(lambda j: s[j], write_strip, lambda j: sm[j],
              (scoefs[0], scoefs[1], scoefs[2], eastward, scoefs[4] > 0.0))

    @pl.loop(0, EARLY)
    def _(g):
        merge(g)

    @pl.loop(EARLY, groups)
    def _(g):
        main(g)
        merge(g)

    wrow = jnp.broadcast_to(rmeta[2:3, :], (SUB, total))
    whi = wrow.astype(BF16).astype(F32)
    w16[...] = jnp.concatenate([whi, wrow - whi], axis=0).astype(BF16)
    rowid = lax.broadcasted_iota(jnp.int32, (LANES, total), 0).astype(F32)
    colid = lax.broadcasted_iota(jnp.int32, (LANES, total), 1).astype(F32)

    @pl.loop(0, total // LANES)
    def _(t):
        rows = pl.ds(pl.multiple_of(t * LANES, LANES), LANES)
        meta = fprm[rows, :]
        hot = (jnp.broadcast_to(meta[:, 5:6], (LANES, total)) == colid).astype(F32).astype(BF16)
        picked = jnp.dot(hot, sphl[...], preferred_element_type=F32).astype(BF16)
        dirs = jnp.broadcast_to(rmeta[0:1, :], (LANES, total))
        same = jnp.broadcast_to(meta[:, 4:5], (LANES, total)) == jnp.broadcast_to(rmeta[1:2, :], (LANES, total))
        for ref, base in ((cph, 0), (cpl, LANES // 2)):
            pick = (dirs + base == rowid).astype(F32).astype(BF16)
            full = jnp.dot(picked, pick, preferred_element_type=F32)
            ref[rows, :] = jnp.where(same, full, 0.0).astype(BF16)

    for j in range(block):
        ld[j] = jnp.zeros((SUB, LANES), F32)

        @pl.loop(0, total // LANES)
        def _(t):
            acc[j, pl.ds(pl.multiple_of(t * LANES, LANES), LANES), :] = jnp.zeros((LANES, LANES), F32)

    def arrive(g):
        @pl.loop(1, n)
        def _(k):
            shuffle(g, k).wait_recv()

        keep_mine(g).wait()

    def split(jp, ks):
        e = jnp.concatenate([r[2 * jp, ks, :], r[2 * jp + 1, ks, :]], axis=1)
        hi = e.astype(BF16)
        return hi, (e - hi.astype(F32)).astype(BF16)

    def accumulate(jp, rows, ks, hi, lo):
        ch, cl = cph[rows, ks], cpl[rows, ks]
        part = (jnp.dot(ch, hi, preferred_element_type=F32) + jnp.dot(cl, hi, preferred_element_type=F32)
                + jnp.dot(ch, lo, preferred_element_type=F32))
        acc[2 * jp, rows, :] += part[:, :LANES]
        acc[2 * jp + 1, rows, :] += part[:, LANES:]

    def weigh(jp, ks, hi, lo):
        wh = jnp.dot(w16[:, ks], hi, preferred_element_type=F32)
        wl = jnp.dot(w16[:, ks], lo, preferred_element_type=F32)
        part = wh[:SUB] + wh[SUB:] + wl[:SUB]
        ld[2 * jp] += part[:, :LANES]
        ld[2 * jp + 1] += part[:, LANES:]

    chunk = total // 3

    @pl.loop(0, groups // 2)
    def _(b):
        arrive(2 * b)
        arrive(2 * b + 1)
        ks = pl.ds(pl.multiple_of(b * 2 * span, 2 * span), 2 * span)

        @pl.loop(0, block // 2)
        def _(jp):
            hi, lo = split(jp, ks)
            weigh(jp, ks, hi, lo)

            @pl.loop(0, 3)
            def _(m):
                accumulate(jp, pl.ds(pl.multiple_of(m * chunk, chunk), chunk), ks, hi, lo)

    tail = pl.ds((groups - 1) * span, span)
    arrive(groups - 1)

    @pl.loop(0, block // 2)
    def _(jp):
        hi, lo = split(jp, tail)
        weigh(jp, tail, hi, lo)

    for j in range(block):
        loading = ld[j]
        ld[j] = loading / (1.0 + loading)

    def back(d):
        mine = pl.ds(pl.multiple_of(d * comps, SUB), comps)
        return pltpu.make_async_remote_copy(
            src_ref=outs.at[mine], dst_ref=out.at[:, pl.ds(pl.multiple_of(me * block, block), block), :],
            send_sem=send2.at[lax.rem(d - me + n, n)], recv_sem=recv2.at[lax.rem(d - me + n, n)],
            device_id={"group": d}, device_id_type=MESH)

    def back_mine():
        mine = pl.ds(pl.multiple_of(me * comps, SUB), comps)
        return pltpu.make_async_copy(
            outs.at[mine], out.at[:, pl.ds(pl.multiple_of(me * block, block), block), :], recv2.at[0])

    flat = outs.reshape(n * comps * block, LANES)

    def finish(d):
        @pl.loop(0, groups)
        def _(b):
            at = pl.multiple_of(d * comps + b * SUB, SUB)
            grow, cap, cosine, sine = spread_columns(fprm, at, 4)
            for j in range(block):
                e = r[j, pl.ds(pl.multiple_of(b * span + d * SUB, SUB), SUB), :]
                u = jnp.broadcast_to(wind[j:j + 1, :], (SUB, LANES))
                v = jnp.broadcast_to(wind[block + j:block + j + 1, :], (SUB, LANES))
                power = grow * relu(cosine * u + sine * v) - cap * ld[j]
                new = e * jnp.exp(power) + 0.5 * acc[j, pl.ds(at, SUB), :]
                flat[pl.ds(d * comps * block + b * SUB * block + j, SUB, stride=block), :] = new * mb[me * block + j]

    quarter = n // 4
    base = lax.div(me, quarter)

    @pl.loop(0, 4)
    def _(c):
        turn = jnp.where(c == 0, 2, jnp.where(c == 1, 1, jnp.where(c == 2, 3, 0)))
        m = lax.rem(base + turn, 4)
        rows = pl.ds(pl.multiple_of(m * quarter * comps, 16), quarter * comps)

        @pl.loop(0, block // 2)
        def _(jp):
            hi, lo = split(jp, tail)
            accumulate(jp, rows, tail, hi, lo)

        @pl.loop(0, quarter)
        def _(i):
            d = m * quarter + i
            finish(d)

            @pl.when(d != me)
            def _():
                back(d).start()

            @pl.when(d == me)
            def _():
                back_mine().start()

    @pl.loop(0, groups)
    def _(g):
        @pl.loop(1, n)
        def _(k):
            shuffle(g, k).wait_send()

    to_east.wait_send()
    to_west.wait_send()

    @pl.loop(1, n)
    def _(k):
        back(lax.rem(me + k, n)).wait()

    back_mine().wait()


def freq_onehot(frequency):
    return (frequency[:, None] == jnp.arange(FREQ)[None, :]).astype(F32)


def local(n, ns, spectrum, land_mask, wind_field, assignment, courant, growth, whitecap, weights, spread):
    me = lax.axis_index("group")
    comps = spectrum.shape[0]
    total = assignment.shape[0]
    groups = comps // SUB
    block = LAT // n
    direction = assignment % DIRS
    frequency = assignment // DIRS
    angles = (direction.astype(F32) + 0.5) * (2.0 * math.pi / DIRS)
    cosine, sine = jnp.cos(angles), jnp.sin(angles)
    table = jnp.stack((growth, whitecap, weights, courant), axis=1)
    picked = jnp.dot(freq_onehot(frequency), table, precision=lax.Precision.HIGHEST)
    fprm = jnp.stack((picked[:, 0], picked[:, 1], cosine, sine, frequency.astype(F32), assignment.astype(F32)), axis=1)
    fprm = jnp.pad(fprm, ((0, 0), (0, LANES - fprm.shape[1])))
    order = jnp.stack((direction.astype(F32), frequency.astype(F32), picked[:, 2] / total))
    rmeta = order.reshape(3, n, groups, SUB).transpose(0, 2, 1, 3).reshape(3, total)
    rmeta = jnp.pad(rmeta, ((0, SUB - 3), (0, 0)))
    fx = picked[:, 3] * cosine
    fy = picked[:, 3] * sine
    mine = jnp.stack((jnp.abs(fx), 1.0 - jnp.abs(fy), jnp.abs(fy), (fx > 0.0).astype(F32), (fy > 0.0).astype(F32)), axis=1)
    mine = lax.dynamic_slice_in_dim(mine, me * comps, comps, 0)
    cprm = jnp.pad(mine, ((0, 0), (0, LANES - 5)))
    sprm = jnp.repeat(mine.reshape(groups, SUB, 5).transpose(2, 1, 0), SLOT, axis=2)
    sprm = jnp.pad(sprm, ((0, 0), (0, 0), (0, LANES - groups * SLOT))).reshape(5 * SUB, LANES)
    rows = spread.reshape(FREQ * DIRS, DIRS)
    high = rows.astype(BF16)
    low = (rows - high.astype(F32)).astype(BF16)
    side = ((0, 0), (0, LANES // 2 - DIRS))
    sphl = jnp.concatenate((jnp.pad(high, side), jnp.pad(low, side)), axis=1)
    latitude = (np.arange(LAT, dtype=np.float64) + 0.5 - LAT / 2) * (math.pi / 2160.0)
    icos = jnp.asarray((1.0 / np.cos(latitude)).astype(np.float32))

    vmem = pl.BlockSpec(memory_space=pltpu.VMEM)
    tiles = lambda count: pltpu.VMEM((count, SUB, LANES), F32)
    dma = pltpu.SemaphoreType.DMA
    call = pl.pallas_call(
        functools.partial(kernel, n, ns, comps),
        out_shape=jax.ShapeDtypeStruct((comps, LAT, LANES), F32),
        in_specs=[pl.BlockSpec(memory_space=pl.ANY), pl.BlockSpec(memory_space=pltpu.SMEM)] + [vmem] * 7,
        out_specs=vmem,
        scratch_shapes=[
            pltpu.VMEM((comps * LAT, LANES), F32),
            pltpu.VMEM((LAT, comps, LANES), F32),
            pltpu.VMEM((block, total, LANES), F32),
            pltpu.VMEM((block, total, LANES), F32),
            pltpu.VMEM((total, total), BF16),
            pltpu.VMEM((total, total), BF16),
            pltpu.VMEM((n * comps, block, LANES), F32),
            tiles(LAT), tiles(LAT // 2), tiles(LAT // 2), tiles(LAT // 2), tiles(LAT // 2),
            tiles(LAT), tiles(LAT), tiles(LAT), tiles(block),
            pltpu.VMEM((2 * SUB, total), BF16),
            dma((groups,)), dma((2,)), dma((2,)),
            dma((groups * n,)), dma((groups * n,)), dma((n,)), dma((n,)),
        ],
        compiler_params=pltpu.CompilerParams(collective_id=0, has_side_effects=True, vmem_limit_bytes=56 << 20),
    )
    return call(spectrum.reshape(comps * LAT, LANES), icos, land_mask, wind_field.reshape(2 * block, LANES),
                cprm, sprm, fprm, rmeta, sphl)


def solution(mesh):
    in_specs = (P("group", None, "sector"), P(None, "sector"), P(None, "group", "sector"), P(), P(), P(), P(), P(), P())
    return jax.shard_map(functools.partial(local, mesh.shape["group"], mesh.shape["sector"]), mesh=mesh,
                         in_specs=in_specs, out_specs=P("group", None, "sector"), check_vma=False)
```

profile of v0, /device:TPU:1, one launch (start us, length us, event | category | flops | bytes accessed | tf_op | source)
XLA Modules:
  0.0 223.9 jit_solution(7598839759793439314)
XLA Ops:
  0.0 0.8 fusion.5
  0.8 1.2 fusion.2
  2.1 0.8 compare_convert_fusion
  2.9 0.8 fusion.7
  3.9 0.1 copy.55
  4.0 0.1 copy.43
  4.1 0.6 pad.23.cprm
  4.9 0.1 copy.47
  5.0 0.1 stack.84
  5.4 0.1 copy.48
  5.5 0.1 reshape.46
  5.6 0.6 pad.26.rmeta
  6.3 0.1 broadcast_in_dim.2
  6.4 0.1 reshape.44
  6.5 0.6 pad_bitcast_fusion.sprm
  7.1 0.2 copy.44
  7.4 0.9 pad.25.fprm
  8.3 0.7 copy.49
  9.0 0.4 reshape.47
  9.4 0.2 copy.50
  9.6 0.3 copy.52
  9.9 0.9 fusion.3.sphl
  10.9 207.9 %shard_map.100 = f32[72,128,128]{2,1,0:T(8,128)} custom-call(f32[9216,128]{1,0:T(8,128)} %bitcast.18, f32[128]{0:T(128)} %constant.45.clone.icos, s32[128,128]{1,0:T(8,128)} %lm.1, f32[16,128]{1,0:T(8,128)} %bitcast.20, f32[72,128]{1,0:T(8,128)} %pad.23.cprm, f32[40,128]{1,0:T(8,128)} %pad_bitcast_fusion.sprm, f32[1152,128]{1,0:T(8,128)} %pad.25.fprm, ...), custom_call_target="tpu_custom_call" | custom-call | tf_op jit(solution)/shard_map/pallas_call | solution.py:434
  218.8 5.1 %copy.57 = f32[72,128,128]{2,1,0:T(8,128)} copy(f32[72,128,128]{2,1,0:T(8,128)} %shard_map.100) | data formatting | bytes 9437184
  (23 shorter events, 0.7 us)
Async XLA Ops:
  0.0 8.3 %copy-start = (f32[32,36,36]{2,0,1:T(8,128)S(1)}, f32[32,36,36]{2,0,1:T(8,128)}, u32[]{:S(2)}) copy-start(f32[32,36,36]{2,0,1:T(8,128)} %param.18) | copy-start | bytes 497668
where the time goes:
time: 225 us; the launch traced here: 224 us
  Pallas kernels  208 us (92%)
  local copies, waits for them, and re-layouts  11.2 us (5%)
  other arithmetic  3.35 us (1%)
    pallas_call x1, Pallas kernels, local(): call(spectrum.reshape(comps * LAT, LANES), icos, land_mask, wind_field.re...  208 us
    unnamed x5, local copies, waits for them, and re-layouts  5.92 us

commit v1 on v0

v1 whole, which is shorter than its diff:
```python
import functools
import math

import jax
import jax.numpy as jnp
import numpy as np
from jax import lax
from jax.experimental import pallas as pl
from jax.experimental.pallas import tpu as pltpu
from jax.sharding import PartitionSpec as P

MESH = pl.DeviceIdType.MESH
DIRS = 36
FREQ = 32
SUBSTEPS = 6
LAT = 128
LANES = 128
EDGE = SUBSTEPS
SLOT = 2 * EDGE
SUB = 8
EARLY = 3
HALVES = 2
PARTS = 4
DEEP = 64
F32 = jnp.float32
BF16 = jnp.bfloat16


def relu(x):
    return jnp.maximum(x, 0.0)


def kernel(n, ns, comps, spec, icos, lm, wind, asg, tabs, sp, out,
           x, p, r, acc, cph, cpl, outs, own, te, tw, ter, twr, s, sm, mb, ld, w16,
           kcol, kq, cpar, spar, fpar, spx,
           land, stage,
           load_sem, halo_send, halo_recv, send1, recv1, mine1, send2, recv2, done):
    me = lax.axis_index("group")
    sec = lax.axis_index("sector")
    east, west = lax.rem(sec + 1, ns), lax.rem(sec + ns - 1, ns)
    total = n * comps
    groups = comps // SUB
    block = LAT // n
    span = n * SUB

    def load(g):
        rows = pl.ds(g * SUB * LAT, SUB * LAT)
        return pltpu.make_async_copy(spec.at[rows], x.at[rows], load_sem.at[g])

    for g in range(groups):
        load(g).start()

    barrier = pltpu.get_barrier_semaphore()

    @pl.loop(1, n)
    def _(k):
        pl.semaphore_signal(barrier, inc=1, device_id={"group": lax.rem(me + k, n)}, device_id_type=MESH)

    for side in (east, west):
        pl.semaphore_signal(barrier, inc=1, device_id={"sector": side}, device_id_type=MESH)

    lane = lax.broadcasted_iota(jnp.int32, (SUB, LANES), 1)
    first = lax.rem(lane, SLOT) < EDGE

    @pl.loop(0, LAT // SUB)
    def _(t):
        for i in range(SUB):
            j = t * SUB + i
            mb[j] = jnp.broadcast_to(lm[pl.ds(j, 1), :].astype(F32), (SUB, LANES))

    @pl.loop(0, total // LANES)
    def _(t):
        row = asg[pl.ds(t, 1), :].astype(F32)
        kcol[pl.ds(pl.multiple_of(t * LANES, LANES), LANES), :] = jnp.broadcast_to(row, (LANES, LANES)).T

    def parts(kind):
        freq = jnp.floor((kind + 0.5) * (1.0 / DIRS))
        return kind - DIRS * freq, freq

    lanef = lane.astype(F32)

    def look(k, index):
        hit = jnp.where(lanef == index, jnp.broadcast_to(tabs[k:k + 1, :], (SUB, LANES)), 0.0)
        return jnp.broadcast_to(jnp.sum(hit, axis=1, keepdims=True), (SUB, LANES))

    strips = [jnp.zeros((SUB, LANES), F32)] * 5
    for g in range(groups):
        direction, freq = parts(kcol[pl.ds(pl.multiple_of(me * comps + g * SUB, SUB), SUB), :])
        speed = look(0, freq)
        fx = speed * look(4, direction)
        fy = speed * look(5, direction)
        values = (jnp.abs(fx), 1.0 - jnp.abs(fy), jnp.abs(fy), (fx > 0.0).astype(F32), (fy > 0.0).astype(F32))
        slot = (lane >= SLOT * g) & (lane < SLOT * (g + 1))
        for k in range(5):
            cpar[g * 5 + k] = values[k]
            strips[k] = jnp.where(slot, values[k], strips[k])
    for k in range(5):
        spar[k] = strips[k]

    for g in range(groups):
        load(g).wait()

    half = LAT // 2

    def window(j):
        packed = pltpu.roll(mb[j], EDGE + SLOT * groups, axis=1)
        for g in range(groups):
            tile = x[pl.ds(g * SUB * LAT + j, SUB, stride=LAT), :]
            tile = pltpu.roll(tile, EDGE + SLOT * g, axis=1)
            packed = jnp.where((lane >= SLOT * g) & (lane < SLOT * (g + 1)), tile, packed)
        return packed

    piece = half // PARTS

    def halo(src, dst, k, c, side):
        rows = pl.ds(c * piece, piece)
        return pltpu.make_async_remote_copy(
            src_ref=src.at[rows], dst_ref=dst.at[rows], send_sem=halo_send.at[k * PARTS + c],
            recv_sem=halo_recv.at[k * PARTS + c], device_id={"sector": side}, device_id_type=MESH)

    def to_east(c):
        return halo(te, ter, 0, c, east)

    def to_west(c):
        return halo(tw, twr, 1, c, west)

    @pl.loop(0, half // 4)
    def _(t):
        rows = [t * 4 + i for i in range(4)]
        lows = [window(j) for j in rows]
        highs = [window(j + half) for j in rows]
        for j, low, high in zip(rows, lows, highs):
            own[j] = low
            own[j + half] = high
            te[j] = jnp.where(first, low, pltpu.roll(high, EDGE, axis=1))
            tw[j] = jnp.where(first, pltpu.roll(high, LANES - EDGE, axis=1), low)

    pl.semaphore_wait(barrier, n + 1)

    @pl.loop(0, PARTS)
    def _(c):
        to_east(c).start()
        to_west(c).start()

    def sweep(read, write, mask, coefs):
        rate, keep, north, sx, sy = coefs

        def rows(j0, prev, cur, nexts):
            tiles = [prev, cur] + nexts
            for i in range(DEEP):
                e = tiles[i + 1]
                fx = jnp.where(sx, pltpu.roll(e, 1, axis=1), pltpu.roll(e, LANES - 1, axis=1))
                fy = jnp.where(sy, tiles[i], tiles[i + 2])
                new = keep * e + north * fy + (rate * icos[j0 + i]) * (fx - e)
                write(j0 + i, new * mask(j0 + i))
            return tiles[DEEP], tiles[DEEP + 1]

        def body(t, carry):
            j0 = t * DEEP
            return rows(j0, *carry, [read(j0 + 1 + i) for i in range(DEEP)])

        zero = jnp.zeros((SUB, LANES), F32)
        prev, cur = lax.fori_loop(0, LAT // DEEP - 1, body, (zero, read(0)))
        j0 = LAT - DEEP
        rows(j0, prev, cur, [read(j0 + 1 + i) for i in range(DEEP - 1)] + [zero])

    def mask_row(j):
        return mb[j]

    def main(g):
        rate, keep, north, sx, sy = [cpar[g * 5 + k] for k in range(5)]
        coefs = (rate, keep, north, sx > 0.0, sy > 0.0)
        mine = pl.ds(pl.multiple_of(g * SUB, SUB), SUB)

        def write(j, v):
            p[j, mine, :] = v

        sweep(lambda j: x[pl.ds(g * SUB * LAT + j, SUB, stride=LAT), :], write, mask_row, coefs)

        @pl.loop(1, SUBSTEPS)
        def _(_k):
            sweep(lambda j: p[j, mine, :], write, mask_row, coefs)

    part = block // HALVES

    def source(g, h, peer):
        return p.at[pl.ds(peer * block + h * part, part), pl.ds(pl.multiple_of(g * SUB, SUB), SUB), :]

    def target(g, h):
        return r.at[pl.ds(h * part, part), pl.ds(pl.multiple_of(g * span + me * SUB, SUB), SUB), :]

    def shuffle(g, h):
        @pl.loop(1, n)
        def _(k):
            peer = lax.rem(me + k, n)
            pltpu.make_async_remote_copy(
                src_ref=source(g, h, peer), dst_ref=target(g, h), send_sem=send1.at[g * HALVES + h],
                recv_sem=recv1.at[g * HALVES + h], device_id={"group": peer}, device_id_type=MESH).start()

        keep_mine(g, h).start()

    def keep_mine(g, h):
        return pltpu.make_async_copy(source(g, h, me), target(g, h), mine1.at[g * HALVES + h])

    def whole(g, h):
        view = r.at[pl.ds(h * part, part), pl.ds(pl.multiple_of(g * span, SUB), span - SUB), :]
        return pltpu.make_async_remote_copy(
            src_ref=view, dst_ref=view, send_sem=send1.at[g * HALVES + h], recv_sem=recv1.at[g * HALVES + h],
            device_id={"group": lax.rem(me + 1, n)}, device_id_type=MESH)

    def arrive(g, h):
        whole(g, h).wait_recv()
        keep_mine(g, h).wait()

    def merge(g):
        seam = jnp.where(cpar[g * 5 + 3] > 0.0, (lane < EDGE).astype(F32), (lane >= LANES - EDGE).astype(F32)) > 0.0
        mine = pl.ds(pl.multiple_of(g * SUB, SUB), SUB)
        shift = LANES - EDGE - SLOT * g

        @pl.loop(0, LAT // SUB)
        def _(t):
            for i in range(SUB):
                j = t * SUB + i
                p[j, mine, :] = jnp.where(seam, pltpu.roll(s[j], shift, axis=1), p[j, mine, :])

        shuffle(g, 0)

    @pl.loop(0, EARLY)
    def _(g):
        main(g)

    scoefs = [spar[k] for k in range(5)]
    eastward = scoefs[3] > 0.0
    lastslot = (lane >= SLOT * groups) & (lane < SLOT * (groups + 1))

    def fan(v):
        v1 = jnp.where(lastslot, v, 0.0)
        v2 = v1 + pltpu.roll(v1, LANES - SLOT, axis=1)
        v4 = v2 + pltpu.roll(v2, LANES - 2 * SLOT, axis=1)
        v8 = v4 + pltpu.roll(v4, LANES - 4 * SLOT, axis=1)
        return v8 + pltpu.roll(v2, LANES - 8 * SLOT, axis=1)

    @pl.loop(0, PARTS)
    def _(c):
        to_east(c).wait_recv()
        to_west(c).wait_recv()

        @pl.loop(0, piece // 8)
        def _(t):
            for i in range(8):
                j = c * piece + t * 8 + i
                fe, fw = ter[j], twr[j]
                for row, ve, vw in ((j, fe, fw), (j + half, pltpu.roll(fe, LANES - EDGE, axis=1), pltpu.roll(fw, EDGE, axis=1))):
                    o = own[row]
                    xe = jnp.where(first, ve, o)
                    xw = jnp.where(first, o, vw)
                    s[row] = jnp.where(eastward, xe, xw)
                    sm[row] = jnp.where(eastward, fan(xe), fan(xw))

    def write_strip(j, v):
        s[j] = v

    @pl.loop(0, SUBSTEPS)
    def _(_k):
        sweep(lambda j: s[j], write_strip, lambda j: sm[j],
              (scoefs[0], scoefs[1], scoefs[2], eastward, scoefs[4] > 0.0))

    @pl.loop(0, EARLY)
    def _(g):
        merge(g)
        shuffle(g, 1)

    @pl.loop(EARLY, groups)
    def _(g):
        main(g)
        merge(g)

    @pl.loop(0, total // SUB)
    def _(t):
        at = pl.ds(pl.multiple_of(t * SUB, SUB), SUB)
        direction, freq = parts(kcol[at, :])
        for k, value in enumerate((look(1, freq), look(2, freq), look(4, direction), look(5, direction))):
            fpar[k, at, :] = value

    for g in range(groups):
        column = jnp.concatenate(
            [kcol[pl.ds(d * comps + g * SUB, SUB), :] for d in range(n)], axis=0)
        kq[:, g * LANES:(g + 1) * LANES] = column.T[:SUB]

    dirq, freqq = parts(kq[...])
    rowid = lax.broadcasted_iota(jnp.int32, (LANES, total), 0).astype(F32)
    colid = lax.broadcasted_iota(jnp.int32, (LANES, total), 1).astype(F32)

    def one_hot(hit):
        return hit.astype(F32).astype(BF16)

    share = tabs[...] * (1.0 / total)
    high = share.astype(BF16).astype(F32)
    both = jnp.concatenate([high, share - high], axis=0).astype(BF16)
    picked = jnp.dot(both, one_hot(jnp.broadcast_to(freqq[0:1], (LANES, total)) == rowid), preferred_element_type=F32)
    w16[...] = jnp.concatenate([jnp.broadcast_to(picked[3:4], (SUB, total)),
                                jnp.broadcast_to(picked[SUB + 3:SUB + 4], (SUB, total))], axis=0).astype(BF16)

    spx[...] = jnp.zeros_like(spx)
    spx[:, 0:DIRS] = sp[...]

    @pl.loop(0, total // LANES)
    def _(t):
        rows = pl.ds(pl.multiple_of(t * LANES, LANES), LANES)
        direction, freq = parts(kcol[rows, :])
        hot = one_hot(jnp.concatenate([direction * FREQ + freq] * (total // LANES), axis=1) == colid)
        same = jnp.concatenate([freq] * (total // LANES), axis=1) == jnp.broadcast_to(freqq[0:1], (LANES, total))
        pick = one_hot(jnp.broadcast_to(dirq[0:1], (LANES, total)) == rowid)
        full = spx[...]
        upper = full.astype(BF16)
        lower = (full - upper.astype(F32)).astype(BF16)
        for ref, table in ((cph, upper), (cpl, lower)):
            chosen = jnp.dot(hot, table, preferred_element_type=F32).astype(BF16)
            wide = jnp.dot(chosen, pick, preferred_element_type=F32)
            ref[rows, :] = jnp.where(same, wide, 0.0).astype(BF16)

    for j in range(block):
        ld[j] = jnp.zeros((SUB, LANES), F32)

        @pl.loop(0, total // LANES)
        def _(t):
            acc[j, pl.ds(pl.multiple_of(t * LANES, LANES), LANES), :] = jnp.zeros((LANES, LANES), F32)

    @pl.loop(EARLY, groups)
    def _(g):
        shuffle(g, 1)

    def split(jp, ks):
        e = jnp.concatenate([r[2 * jp, ks, :], r[2 * jp + 1, ks, :]], axis=1)
        hi = e.astype(BF16)
        return hi, (e - hi.astype(F32)).astype(BF16)

    def accumulate(jp, rows, ks, hi, lo):
        ch, cl = cph[rows, ks], cpl[rows, ks]
        part = (jnp.dot(ch, hi, preferred_element_type=F32) + jnp.dot(cl, hi, preferred_element_type=F32)
                + jnp.dot(ch, lo, preferred_element_type=F32))
        acc[2 * jp, rows, :] += part[:, :LANES]
        acc[2 * jp + 1, rows, :] += part[:, LANES:]

    def weigh(jp, ks, hi, lo):
        wh = jnp.dot(w16[:, ks], hi, preferred_element_type=F32)
        wl = jnp.dot(w16[:, ks], lo, preferred_element_type=F32)
        part = wh[:SUB] + wh[SUB:] + wl[:SUB]
        ld[2 * jp] += part[:, :LANES]
        ld[2 * jp + 1] += part[:, LANES:]

    chunk = total // 3

    tail = pl.ds((groups - 1) * span, span)
    quarter = n // 4
    base = lax.div(me, quarter)
    landed = lambda q, h: pl.ds(q * block + h * part, part)

    def sent(h, d):
        return outs.at[pl.ds((h * n + d) * part, part)]

    def back(h, d):
        k = h * n + lax.rem(d - me + n, n)
        return pltpu.make_async_remote_copy(
            src_ref=sent(h, d), dst_ref=land.at[landed(me, h)], send_sem=send2.at[k], recv_sem=recv2.at[k],
            device_id={"group": d}, device_id_type=MESH)

    def back_mine(h):
        return pltpu.make_async_copy(sent(h, me), land.at[landed(me, h)], recv2.at[h * n])

    def finish(h, d):
        @pl.loop(0, groups // 3)
        def _(t):
            for i in range(3):
                b = t * 3 + i
                at = pl.multiple_of(d * comps + b * SUB, SUB)
                grow, cap, cosine, sine = [fpar[k, pl.ds(at, SUB), :] for k in range(4)]
                for jr in range(part):
                    j = h * part + jr
                    e = r[j, pl.ds(pl.multiple_of(b * span + d * SUB, SUB), SUB), :]
                    u = jnp.broadcast_to(wind[pl.ds(j, 1), :], (SUB, LANES))
                    v = jnp.broadcast_to(wind[pl.ds(block + j, 1), :], (SUB, LANES))
                    power = grow * relu(cosine * u + sine * v) - cap * ld[j]
                    new = e * jnp.exp(power) + 0.5 * acc[j, pl.ds(at, SUB), :]
                    outs[(h * n + d) * part + jr, pl.ds(pl.multiple_of(b * SUB, SUB), SUB), :] = new * mb[me * block + j]

    def turn(c):
        return jnp.where(c == 0, 2, jnp.where(c == 1, 1, jnp.where(c == 2, 3, 0)))

    @pl.loop(0, HALVES)
    def _(h):
        pairs = part // 2

        @pl.loop(0, groups // 2)
        def _(b):
            arrive(2 * b, h)
            arrive(2 * b + 1, h)
            ks = pl.ds(pl.multiple_of(b * 2 * span, 2 * span), 2 * span)

            @pl.loop(0, pairs)
            def _(i):
                jp = h * pairs + i
                hi, lo = split(jp, ks)
                weigh(jp, ks, hi, lo)

                @pl.loop(0, 3)
                def _(m):
                    accumulate(jp, pl.ds(pl.multiple_of(m * chunk, chunk), chunk), ks, hi, lo)

        arrive(groups - 1, h)

        @pl.loop(0, pairs)
        def _(i):
            jp = h * pairs + i
            hi, lo = split(jp, tail)
            weigh(jp, tail, hi, lo)

        for jr in range(part):
            j = h * part + jr
            loading = ld[j]
            ld[j] = loading / (1.0 + loading)

        @pl.loop(0, 4)
        def _(c):
            m = lax.rem(base + turn(c), 4)
            rows = pl.ds(pl.multiple_of(m * quarter * comps, 16), quarter * comps)

            @pl.loop(0, pairs)
            def _(i):
                jp = h * pairs + i
                hi, lo = split(jp, tail)
                accumulate(jp, rows, tail, hi, lo)

            @pl.loop(0, quarter)
            def _(i):
                d = m * quarter + i
                finish(h, d)

                @pl.when(d != me)
                def _():
                    back(h, d).start()

                @pl.when(d == me)
                def _():
                    back_mine(h).start()

    @pl.loop(0, groups)
    def _(g):
        for h in range(HALVES):
            whole(g, h).wait_send()

    @pl.loop(0, PARTS)
    def _(c):
        to_east(c).wait_send()
        to_west(c).wait_send()

    flat = stage.reshape(n * comps * block, LANES)

    def deliver(q):
        return pltpu.make_async_copy(
            stage.at[pl.ds(pl.multiple_of(q * comps, SUB), comps)],
            out.at[:, pl.ds(pl.multiple_of(q * block, block), block), :], done.at[q])

    def relayout(q):
        @pl.loop(0, groups // 3)
        def _(t):
            for i in range(3):
                b = t * 3 + i
                for j in range(block):
                    flat[pl.ds((q * comps + b * SUB) * block + j, SUB, stride=block), :] = (
                        land[q * block + j, pl.ds(pl.multiple_of(b * SUB, SUB), SUB), :])

        deliver(q).start()

    @pl.loop(0, 4)
    def _(c):
        m = lax.rem(base + 4 - turn(c), 4)

        @pl.loop(0, quarter)
        def _(i):
            q = m * quarter + i
            k = lax.rem(me - q + n, n)

            @pl.when(q != me)
            def _():
                for h in range(HALVES):
                    back(h, lax.rem(me + k, n)).wait_recv()

            @pl.when(q == me)
            def _():
                for h in range(HALVES):
                    back_mine(h).wait()

            relayout(q)

    @pl.loop(1, n)
    def _(k):
        for h in range(HALVES):
            back(h, lax.rem(me + k, n)).wait_send()

    @pl.loop(0, n)
    def _(q):
        deliver(q).wait()


def local(n, ns, spectrum, land_mask, wind_field, assignment, courant, growth, whitecap, weights, spread):
    comps = spectrum.shape[0]
    total = assignment.shape[0]
    groups = comps // SUB
    block = LAT // n
    turns = np.zeros((4, LANES), np.float32)
    angles = (np.arange(DIRS) + 0.5) * (2.0 * math.pi / DIRS)
    turns[0, :DIRS] = np.cos(angles)
    turns[1, :DIRS] = np.sin(angles)
    tables = jnp.pad(jnp.stack((courant, growth, whitecap, weights)), ((0, 0), (0, LANES - FREQ)))
    tabs = jnp.concatenate((tables, jnp.asarray(turns)))
    latitude = (np.arange(LAT, dtype=np.float64) + 0.5 - LAT / 2) * (math.pi / 2160.0)
    icos = jnp.asarray((1.0 / np.cos(latitude)).astype(np.float32))

    vmem = pl.BlockSpec(memory_space=pltpu.VMEM)
    tiles = lambda count: pltpu.VMEM((count, SUB, LANES), F32)
    dma = pltpu.SemaphoreType.DMA
    call = pl.pallas_call(
        functools.partial(kernel, n, ns, comps),
        out_shape=jax.ShapeDtypeStruct((comps, LAT, LANES), F32),
        in_specs=[pl.BlockSpec(memory_space=pltpu.HBM), pl.BlockSpec(memory_space=pltpu.SMEM)] + [vmem] * 5,
        out_specs=pl.BlockSpec(memory_space=pl.ANY),
        scratch_shapes=[
            pltpu.VMEM((comps * LAT, LANES), F32),
            pltpu.VMEM((LAT, comps, LANES), F32),
            pltpu.VMEM((block, total, LANES), F32),
            pltpu.VMEM((block, total, LANES), F32),
            pltpu.VMEM((total, total), BF16),
            pltpu.VMEM((total, total), BF16),
            pltpu.VMEM((n * block, comps, LANES), F32),
            tiles(LAT), tiles(LAT // 2), tiles(LAT // 2), tiles(LAT // 2), tiles(LAT // 2),
            tiles(LAT), tiles(LAT), tiles(LAT), tiles(block),
            pltpu.VMEM((2 * SUB, total), BF16),
            pltpu.VMEM((total, LANES), F32),
            pltpu.VMEM((SUB, total), F32),
            tiles(groups * 5), tiles(5),
            pltpu.VMEM((4, total, LANES), F32),
            pltpu.VMEM((total, LANES), F32),
            pltpu.VMEM((LAT, comps, LANES), F32),
            pltpu.VMEM((n * comps, block, LANES), F32),
            dma((groups,)), dma((2 * PARTS,)), dma((2 * PARTS,)),
            dma((groups * HALVES,)), dma((groups * HALVES,)), dma((groups * HALVES,)),
            dma((HALVES * n,)), dma((HALVES * n,)), dma((n,)),
        ],
        compiler_params=pltpu.CompilerParams(collective_id=0, has_side_effects=True, vmem_limit_bytes=48 << 20),
    )
    return call(spectrum.reshape(comps * LAT, LANES), icos, land_mask, wind_field.reshape(2 * block, LANES),
                assignment.reshape(total // LANES, LANES), tabs, spread.transpose(1, 0, 2).reshape(FREQ * DIRS, DIRS))


def solution(mesh):
    in_specs = (P("group", None, "sector"), P(None, "sector"), P(None, "group", "sector"), P(), P(), P(), P(), P(), P())
    return jax.shard_map(functools.partial(local, mesh.shape["group"], mesh.shape["sector"]), mesh=mesh,
                         in_specs=in_specs, out_specs=P("group", None, "sector"), check_vma=False)
```

time: 225 us -> 150 us (0.67)
  Pallas kernels: 208 us -> 143 us
  local copies, waits for them, and re-layouts: 11.2 us -> 6.14 us
    pallas_call x1, Pallas kernels: 208 us -> 143 us  [local(): call(spectrum.reshape(comps * LAT, LANES), icos, land_mask, wind_field.re...]
    unnamed x5 -> x11, local copies, waits for them, and re-layouts: 5.92 us -> 6.14 us
where the time goes in v1:
time: 150 us
  Pallas kernels  143 us (95%)
  local copies, waits for them, and re-layouts  6.14 us (4%)
    pallas_call x1, Pallas kernels, local(): call(spectrum.reshape(comps * LAT, LANES), icos, land_mask, wind_field.re...  143 us
    unnamed x11, local copies, waits for them, and re-layouts  6.14 us

profile of v1, /device:TPU:1, one launch (start us, length us, event | category | flops | bytes accessed | tf_op | source)
XLA Modules:
  0.0 150.1 jit_solution(9546913887917862438)
XLA Ops:
  0.0 0.7 select_maximum_fusion
  0.7 0.7 pad_maximum_fusion.tabs
  1.4 0.0 copy-start
  1.4 1.1 copy-done
  2.5 0.0 copy-start.1
  2.5 0.8 copy-done.1
  3.3 0.0 copy-start.2
  3.3 0.7 copy-done.2
  4.0 0.0 copy-start.3
  4.0 0.7 copy-done.3
  4.7 0.0 copy-start.4
  4.7 0.7 copy-done.4
  5.4 142.5 %shard_map.109 = f32[72,128,128]{2,1,0:T(8,128)S(1)} custom-call(f32[9216,128]{1,0:T(8,128)} %bitcast.13, f32[128]{0:T(128)S(1)} %copy-done.4, s32[128,128]{1,0:T(8,128)S(1)} %copy-done.1, f32[16,128]{1,0:T(8,128)S(1)} %bitcast.11, s32[9,128]{1,0:T(8,128)S(1)} %bitcast.12, f32[8,128]{1,0:T(8,128)S(1)} %pad_maximum_fusion.tabs, f32[1152,36]{1,0:T(8,128)S(1)} %bitcast.10), custom_call_target="tpu_custom_call" | custom-call | tf_op jit(solution)/shard_map/pallas_call | solution.py:552
  147.9 2.2 %copy.13 = f32[72,128,128]{2,1,0:T(8,128)} copy(f32[72,128,128]{2,1,0:T(8,128)S(1)} %shard_map.109) | data formatting | bytes 9437184
Async XLA Ops:
  1.4 1.1 copy-start
  2.5 0.8 copy-start.1
  3.3 0.7 copy-start.2
  4.0 0.7 copy-start.3
  4.7 0.7 copy-start.4

commit v2 on v1

--- a/solution.py
+++ b/solution.py
@@ -20,7 +20,7 @@
 SUB = 8
 EARLY = 3
 HALVES = 2
-PARTS = 4
+PARTS = 3
 DEEP = 64
 F32 = jnp.float32
 BF16 = jnp.bfloat16
@@ -30,11 +30,15 @@
     return jnp.maximum(x, 0.0)
 
 
-def kernel(n, ns, comps, spec, icos, lm, wind, asg, tabs, sp, out,
-           x, p, r, acc, cph, cpl, outs, own, te, tw, ter, twr, s, sm, mb, ld, w16,
+def kernel(n, ns, comps, spec, small, sp, out,
+           x, p, r, acc, cph, cpl, outs, own, te, tw, ter, twr, s, sm, mb, ld, w16, icos,
            kcol, kq, cpar, spar, fpar, spx,
            land, stage,
            load_sem, halo_send, halo_recv, send1, recv1, mine1, send2, recv2, done):
+    lm = small.at[pl.ds(0, LAT)]
+    wind = small.at[pl.ds(LAT, 2 * SUB)]
+    tabs = small.at[pl.ds(LAT + 2 * SUB, SUB)]
+    asg = small.at[pl.ds(LAT + 3 * SUB, n)]
     me = lax.axis_index("group")
     sec = lax.axis_index("sector")
     east, west = lax.rem(sec + 1, ns), lax.rem(sec + ns - 1, ns)
@@ -50,6 +54,9 @@
     for g in range(groups):
         load(g).start()
 
+    for j in range(LAT):
+        icos[j] = np.float32(1.0 / math.cos((j + 0.5 - LAT / 2) * (math.pi / 2160.0)))
+
     barrier = pltpu.get_barrier_semaphore()
 
     @pl.loop(1, n)
@@ -66,11 +73,11 @@
     def _(t):
         for i in range(SUB):
             j = t * SUB + i
-            mb[j] = jnp.broadcast_to(lm[pl.ds(j, 1), :].astype(F32), (SUB, LANES))
+            mb[j] = jnp.broadcast_to(lm[pl.ds(j, 1), :], (SUB, LANES))
 
     @pl.loop(0, total // LANES)
     def _(t):
-        row = asg[pl.ds(t, 1), :].astype(F32)
+        row = asg[pl.ds(t, 1), :]
         kcol[pl.ds(pl.multiple_of(t * LANES, LANES), LANES), :] = jnp.broadcast_to(row, (LANES, LANES)).T
 
     def parts(kind):
@@ -79,41 +86,74 @@
 
     lanef = lane.astype(F32)
 
+    tables = [jnp.broadcast_to(tabs[k:k + 1, :], (SUB, LANES)) for k in range(4)]
+    for wave in (math.cos, math.sin):
+        values = jnp.zeros((SUB, LANES), F32)
+        for d in range(DIRS):
+            values = jnp.where(lane == d, np.float32(wave((d + 0.5) * (2.0 * math.pi / DIRS))), values)
+        tables.append(values)
+
     def look(k, index):
-        hit = jnp.where(lanef == index, jnp.broadcast_to(tabs[k:k + 1, :], (SUB, LANES)), 0.0)
+        hit = jnp.where(lanef == index, tables[k], 0.0)
         return jnp.broadcast_to(jnp.sum(hit, axis=1, keepdims=True), (SUB, LANES))
 
-    strips = [jnp.zeros((SUB, LANES), F32)] * 5
+    sets = [list(range(EARLY)), list(range(EARLY, groups))]
+    strips = [[jnp.zeros((SUB, LANES), F32)] * 5 for _ in sets]
     for g in range(groups):
+        which = 0 if g < EARLY else 1
+        place = g - sets[which][0]
         direction, freq = parts(kcol[pl.ds(pl.multiple_of(me * comps + g * SUB, SUB), SUB), :])
         speed = look(0, freq)
         fx = speed * look(4, direction)
         fy = speed * look(5, direction)
         values = (jnp.abs(fx), 1.0 - jnp.abs(fy), jnp.abs(fy), (fx > 0.0).astype(F32), (fy > 0.0).astype(F32))
-        slot = (lane >= SLOT * g) & (lane < SLOT * (g + 1))
+        slot = (lane >= SLOT * place) & (lane < SLOT * (place + 1))
         for k in range(5):
             cpar[g * 5 + k] = values[k]
-            strips[k] = jnp.where(slot, values[k], strips[k])
-    for k in range(5):
-        spar[k] = strips[k]
+            strips[which][k] = jnp.where(slot, values[k], strips[which][k])
+    for which in range(2):
+        for k in range(5):
+            spar[which * 5 + k] = strips[which][k]
 
     for g in range(groups):
         load(g).wait()
 
     half = LAT // 2
-
-    def window(j):
-        packed = pltpu.roll(mb[j], EDGE + SLOT * groups, axis=1)
-        for g in range(groups):
+    fourth = half // 2
+    fold = SLOT * (EARLY + 1)
+
+    def window(members, j):
+        packed = pltpu.roll(mb[j], EDGE + SLOT * len(members), axis=1)
+        for i, g in enumerate(members):
             tile = x[pl.ds(g * SUB * LAT + j, SUB, stride=LAT), :]
-            tile = pltpu.roll(tile, EDGE + SLOT * g, axis=1)
-            packed = jnp.where((lane >= SLOT * g) & (lane < SLOT * (g + 1)), tile, packed)
+            tile = pltpu.roll(tile, EDGE + SLOT * i, axis=1)
+            packed = jnp.where((lane >= SLOT * i) & (lane < SLOT * (i + 1)), tile, packed)
         return packed
 
-    piece = half // PARTS
+    def pair(which, j):
+        low, high = window(sets[which], j), window(sets[which], j + half)
+        own[which * LAT + j] = low
+        own[which * LAT + j + half] = high
+        return (jnp.where(first, low, pltpu.roll(high, EDGE, axis=1)),
+                jnp.where(first, pltpu.roll(high, LANES - EDGE, axis=1), low))
+
+    def folded(a, b):
+        return jnp.where(lane < fold, a, pltpu.roll(b, fold, axis=1))
+
+    @pl.loop(0, fourth // 4)
+    def _(t):
+        for i in range(4):
+            j = t * 4 + i
+            ea, wa = pair(0, j)
+            eb, wb = pair(0, j + fourth)
+            te[j] = folded(ea, eb)
+            tw[j] = folded(wa, wb)
+
+    pl.semaphore_wait(barrier, n + 1)
+    starts = [0, fourth, fourth + half // 2, fourth + half]
 
     def halo(src, dst, k, c, side):
-        rows = pl.ds(c * piece, piece)
+        rows = pl.ds(starts[c], starts[c + 1] - starts[c])
         return pltpu.make_async_remote_copy(
             src_ref=src.at[rows], dst_ref=dst.at[rows], send_sem=halo_send.at[k * PARTS + c],
             recv_sem=halo_recv.at[k * PARTS + c], device_id={"sector": side}, device_id_type=MESH)
@@ -124,21 +164,16 @@
     def to_west(c):
         return halo(tw, twr, 1, c, west)
 
+    to_east(0).start()
+    to_west(0).start()
+
     @pl.loop(0, half // 4)
     def _(t):
-        rows = [t * 4 + i for i in range(4)]
-        lows = [window(j) for j in rows]
-        highs = [window(j + half) for j in rows]
-        for j, low, high in zip(rows, lows, highs):
-            own[j] = low
-            own[j + half] = high
-            te[j] = jnp.where(first, low, pltpu.roll(high, EDGE, axis=1))
-            tw[j] = jnp.where(first, pltpu.roll(high, LANES - EDGE, axis=1), low)
-
-    pl.semaphore_wait(barrier, n + 1)
-
-    @pl.loop(0, PARTS)
-    def _(c):
+        for i in range(4):
+            j = t * 4 + i
+            te[fourth + j], tw[fourth + j] = pair(1, j)
+
+    for c in (1, 2):
         to_east(c).start()
         to_west(c).start()
 
@@ -212,75 +247,103 @@
         whole(g, h).wait_recv()
         keep_mine(g, h).wait()
 
-    def merge(g):
+    def merge(g, origin):
         seam = jnp.where(cpar[g * 5 + 3] > 0.0, (lane < EDGE).astype(F32), (lane >= LANES - EDGE).astype(F32)) > 0.0
         mine = pl.ds(pl.multiple_of(g * SUB, SUB), SUB)
-        shift = LANES - EDGE - SLOT * g
-
-        @pl.loop(0, LAT // SUB)
+        shift = LANES - EDGE - SLOT * (g - origin)
+
+        @pl.loop(0, LAT // (2 * SUB))
         def _(t):
-            for i in range(SUB):
-                j = t * SUB + i
+            for i in range(2 * SUB):
+                j = t * 2 * SUB + i
                 p[j, mine, :] = jnp.where(seam, pltpu.roll(s[j], shift, axis=1), p[j, mine, :])
 
         shuffle(g, 0)
+
+    def fan(v, last):
+        v1 = jnp.where((lane >= SLOT * last) & (lane < SLOT * (last + 1)), v, 0.0)
+        v2 = v1 + pltpu.roll(v1, LANES - SLOT, axis=1)
+        v4 = v2 + pltpu.roll(v2, LANES - 2 * SLOT, axis=1)
+        return v4 if last < 4 else v4 + pltpu.roll(v4, LANES - 4 * SLOT, axis=1)
+
+    def unpack(which, pairs):
+        last = len(sets[which])
+        eastward = spar[which * 5 + 3] > 0.0
+        for j, fe, fw in pairs:
+            for row, ve, vw in ((j, fe, fw), (j + half, pltpu.roll(fe, LANES - EDGE, axis=1), pltpu.roll(fw, EDGE, axis=1))):
+                o = own[which * LAT + row]
+                xe = jnp.where(first, ve, o)
+                xw = jnp.where(first, o, vw)
+                s[row] = jnp.where(eastward, xe, xw)
+                sm[row] = jnp.where(eastward, fan(xe, last), fan(xw, last))
+
+    def write_strip(j, v):
+        s[j] = v
+
+    def strips_of(which):
+        scoefs = [spar[which * 5 + k] for k in range(5)]
+
+        @pl.loop(0, SUBSTEPS)
+        def _(_k):
+            sweep(lambda j: s[j], write_strip, lambda j: sm[j],
+                  (scoefs[0], scoefs[1], scoefs[2], scoefs[3] > 0.0, scoefs[4] > 0.0))
 
     @pl.loop(0, EARLY)
     def _(g):
         main(g)
 
-    scoefs = [spar[k] for k in range(5)]
-    eastward = scoefs[3] > 0.0
-    lastslot = (lane >= SLOT * groups) & (lane < SLOT * (groups + 1))
-
-    def fan(v):
-        v1 = jnp.where(lastslot, v, 0.0)
-        v2 = v1 + pltpu.roll(v1, LANES - SLOT, axis=1)
-        v4 = v2 + pltpu.roll(v2, LANES - 2 * SLOT, axis=1)
-        v8 = v4 + pltpu.roll(v4, LANES - 4 * SLOT, axis=1)
-        return v8 + pltpu.roll(v2, LANES - 8 * SLOT, axis=1)
-
-    @pl.loop(0, PARTS)
-    def _(c):
+    to_east(0).wait_recv()
+    to_west(0).wait_recv()
+
+    @pl.loop(0, fourth // 4)
+    def _(t):
+        pairs = []
+        for i in range(4):
+            j = t * 4 + i
+            fe, fw = ter[j], twr[j]
+            pairs.append((j, fe, fw))
+            pairs.append((j + fourth, pltpu.roll(fe, LANES - fold, axis=1), pltpu.roll(fw, LANES - fold, axis=1)))
+        unpack(0, pairs)
+
+    strips_of(0)
+
+    @pl.loop(0, EARLY)
+    def _(g):
+        merge(g, 0)
+        shuffle(g, 1)
+
+    @pl.loop(EARLY, EARLY + 1)
+    def _(g):
+        main(g)
+
+    for c in (1, 2):
         to_east(c).wait_recv()
         to_west(c).wait_recv()
 
-        @pl.loop(0, piece // 8)
+        @pl.loop(0, half // 16)
         def _(t):
-            for i in range(8):
-                j = c * piece + t * 8 + i
-                fe, fw = ter[j], twr[j]
-                for row, ve, vw in ((j, fe, fw), (j + half, pltpu.roll(fe, LANES - EDGE, axis=1), pltpu.roll(fw, EDGE, axis=1))):
-                    o = own[row]
-                    xe = jnp.where(first, ve, o)
-                    xw = jnp.where(first, o, vw)
-                    s[row] = jnp.where(eastward, xe, xw)
-                    sm[row] = jnp.where(eastward, fan(xe), fan(xw))
-
-    def write_strip(j, v):
-        s[j] = v
-
-    @pl.loop(0, SUBSTEPS)
-    def _(_k):
-        sweep(lambda j: s[j], write_strip, lambda j: sm[j],
-              (scoefs[0], scoefs[1], scoefs[2], eastward, scoefs[4] > 0.0))
-
-    @pl.loop(0, EARLY)
+            rows = [(c - 1) * (half // 2) + t * 8 + i for i in range(8)]
+            unpack(1, [(j, ter[fourth + j], twr[fourth + j]) for j in rows])
+
+    strips_of(1)
+    merge(EARLY, EARLY)
+
+    @pl.loop(EARLY + 1, groups)
     def _(g):
-        merge(g)
-        shuffle(g, 1)
+        main(g)
+        merge(g, EARLY)
 
     @pl.loop(EARLY, groups)
     def _(g):
-        main(g)
-        merge(g)
-
-    @pl.loop(0, total // SUB)
+        shuffle(g, 1)
+
+    @pl.loop(0, total // (SUB * SUB))
     def _(t):
-        at = pl.ds(pl.multiple_of(t * SUB, SUB), SUB)
-        direction, freq = parts(kcol[at, :])
-        for k, value in enumerate((look(1, freq), look(2, freq), look(4, direction), look(5, direction))):
-            fpar[k, at, :] = value
+        tiles = [pl.ds(pl.multiple_of(t * SUB * SUB + i * SUB, SUB), SUB) for i in range(SUB)]
+        kinds = [parts(kcol[at, :]) for at in tiles]
+        for at, (direction, freq) in zip(tiles, kinds):
+            for k, value in enumerate((look(1, freq), look(2, freq), look(4, direction), look(5, direction))):
+                fpar[k, at, :] = value
 
     for g in range(groups):
         column = jnp.concatenate(
@@ -294,7 +357,7 @@
     def one_hot(hit):
         return hit.astype(F32).astype(BF16)
 
-    share = tabs[...] * (1.0 / total)
+    share = tabs[0:SUB, :] * (1.0 / total)
     high = share.astype(BF16).astype(F32)
     both = jnp.concatenate([high, share - high], axis=0).astype(BF16)
     picked = jnp.dot(both, one_hot(jnp.broadcast_to(freqq[0:1], (LANES, total)) == rowid), preferred_element_type=F32)
@@ -325,10 +388,6 @@
         @pl.loop(0, total // LANES)
         def _(t):
             acc[j, pl.ds(pl.multiple_of(t * LANES, LANES), LANES), :] = jnp.zeros((LANES, LANES), F32)
-
-    @pl.loop(EARLY, groups)
-    def _(g):
-        shuffle(g, 1)
 
     def split(jp, ks):
         e = jnp.concatenate([r[2 * jp, ks, :], r[2 * jp + 1, ks, :]], axis=1)
@@ -449,8 +508,7 @@
         for h in range(HALVES):
             whole(g, h).wait_send()
 
-    @pl.loop(0, PARTS)
-    def _(c):
+    for c in range(PARTS):
         to_east(c).wait_send()
         to_west(c).wait_send()
 
@@ -508,22 +566,19 @@
     total = assignment.shape[0]
     groups = comps // SUB
     block = LAT // n
-    turns = np.zeros((4, LANES), np.float32)
-    angles = (np.arange(DIRS) + 0.5) * (2.0 * math.pi / DIRS)
-    turns[0, :DIRS] = np.cos(angles)
-    turns[1, :DIRS] = np.sin(angles)
-    tables = jnp.pad(jnp.stack((courant, growth, whitecap, weights)), ((0, 0), (0, LANES - FREQ)))
-    tabs = jnp.concatenate((tables, jnp.asarray(turns)))
-    latitude = (np.arange(LAT, dtype=np.float64) + 0.5 - LAT / 2) * (math.pi / 2160.0)
-    icos = jnp.asarray((1.0 / np.cos(latitude)).astype(np.float32))
-
+    small = jnp.concatenate((
+        land_mask.astype(F32),
+        wind_field.reshape(2 * block, LANES),
+        jnp.pad(jnp.stack((courant, growth, whitecap, weights)), ((0, SUB - 4), (0, LANES - FREQ))),
+        jnp.pad(assignment.astype(F32).reshape(total // LANES, LANES), ((0, n - total // LANES), (0, 0))),
+    ))
     vmem = pl.BlockSpec(memory_space=pltpu.VMEM)
     tiles = lambda count: pltpu.VMEM((count, SUB, LANES), F32)
     dma = pltpu.SemaphoreType.DMA
     call = pl.pallas_call(
         functools.partial(kernel, n, ns, comps),
         out_shape=jax.ShapeDtypeStruct((comps, LAT, LANES), F32),
-        in_specs=[pl.BlockSpec(memory_space=pltpu.HBM), pl.BlockSpec(memory_space=pltpu.SMEM)] + [vmem] * 5,
+        in_specs=[pl.BlockSpec(memory_space=pl.ANY)] + [vmem] * 2,
         out_specs=pl.BlockSpec(memory_space=pl.ANY),
         scratch_shapes=[
             pltpu.VMEM((comps * LAT, LANES), F32),
@@ -533,12 +588,13 @@
             pltpu.VMEM((total, total), BF16),
             pltpu.VMEM((total, total), BF16),
             pltpu.VMEM((n * block, comps, LANES), F32),
-            tiles(LAT), tiles(LAT // 2), tiles(LAT // 2), tiles(LAT // 2), tiles(LAT // 2),
+            tiles(2 * LAT), tiles(LAT), tiles(LAT), tiles(LAT), tiles(LAT),
             tiles(LAT), tiles(LAT), tiles(LAT), tiles(block),
             pltpu.VMEM((2 * SUB, total), BF16),
+            pltpu.SMEM((LAT,), F32),
             pltpu.VMEM((total, LANES), F32),
             pltpu.VMEM((SUB, total), F32),
-            tiles(groups * 5), tiles(5),
+            tiles(groups * 5), tiles(10),
             pltpu.VMEM((4, total, LANES), F32),
             pltpu.VMEM((total, LANES), F32),
             pltpu.VMEM((LAT, comps, LANES), F32),
@@ -549,8 +605,7 @@
         ],
         compiler_params=pltpu.CompilerParams(collective_id=0, has_side_effects=True, vmem_limit_bytes=48 << 20),
     )
-    return call(spectrum.reshape(comps * LAT, LANES), icos, land_mask, wind_field.reshape(2 * block, LANES),
-                assignment.reshape(total // LANES, LANES), tabs, spread.transpose(1, 0, 2).reshape(FREQ * DIRS, DIRS))
+    return call(spectrum.reshape(comps * LAT, LANES), small, spread.transpose(1, 0, 2).reshape(FREQ * DIRS, DIRS))
 
 
 def solution(mesh):

time: 150 us -> 136 us (0.907)
  Pallas kernels: 143 us -> 130 us
  local copies, waits for them, and re-layouts: 6.14 us -> 3.25 us
  other arithmetic: 1.41 us -> 2.97 us
    pallas_call x1, Pallas kernels: 143 us -> 130 us  [local(): call(spectrum.reshape(comps * LAT, LANES), small, spread.transpose(1, 0,...]
    unnamed x11 -> x3, local copies, waits for them, and re-layouts: 6.14 us -> 3.25 us
where the time goes in v2:
time: 136 us
  Pallas kernels  130 us (96%)
  local copies, waits for them, and re-layouts  3.25 us (2%)
  other arithmetic  2.97 us (2%)
    pallas_call x1, Pallas kernels, local(): call(spectrum.reshape(comps * LAT, LANES), small, spread.transpose(1, 0,...  130 us
    unnamed x3, local copies, waits for them, and re-layouts  3.25 us

profile of v2, /device:TPU:1, one launch (start us, length us, event | category | flops | bytes accessed | tf_op | source)
XLA Modules:
  0.0 135.9 jit_solution(14529319033393840753)
XLA Ops:
  0.0 0.7 select_maximum_fusion.1
  0.7 0.7 convert_bitcast_fusion
  1.4 0.8 convert_element_type.10
  2.3 0.7 select_maximum_fusion.small
  3.0 0.0 copy-start
  3.0 1.1 copy-done
  4.0 129.7 %shard_map.91 = f32[72,128,128]{2,1,0:T(8,128)S(1)} custom-call(f32[9216,128]{1,0:T(8,128)} %bitcast.12, f32[168,128]{1,0:T(8,128)S(1)} %select_maximum_fusion.small, f32[1152,36]{1,0:T(8,128)S(1)} %bitcast.11), custom_call_target="tpu_custom_call" | custom-call | tf_op jit(solution)/shard_map/pallas_call | solution.py:608
  133.7 2.2 %copy.11 = f32[72,128,128]{2,1,0:T(8,128)} copy(f32[72,128,128]{2,1,0:T(8,128)S(1)} %shard_map.91) | data formatting | bytes 9437184
Async XLA Ops:
  3.0 1.1 copy-start

commit v3 on v2

--- a/solution.py
+++ b/solution.py
@@ -18,7 +18,7 @@
 EDGE = SUBSTEPS
 SLOT = 2 * EDGE
 SUB = 8
-EARLY = 3
+EARLY = 2
 HALVES = 2
 PARTS = 3
 DEEP = 64
@@ -30,15 +30,15 @@
     return jnp.maximum(x, 0.0)
 
 
-def kernel(n, ns, comps, spec, small, sp, out,
+def kernel(n, ns, comps, spec, whole_small, part_small, sp, out,
            x, p, r, acc, cph, cpl, outs, own, te, tw, ter, twr, s, sm, mb, ld, w16, icos,
            kcol, kq, cpar, spar, fpar, spx,
            land, stage,
            load_sem, halo_send, halo_recv, send1, recv1, mine1, send2, recv2, done):
-    lm = small.at[pl.ds(0, LAT)]
-    wind = small.at[pl.ds(LAT, 2 * SUB)]
-    tabs = small.at[pl.ds(LAT + 2 * SUB, SUB)]
-    asg = small.at[pl.ds(LAT + 3 * SUB, n)]
+    lm = whole_small.at[pl.ds(0, LAT)]
+    asg = whole_small.at[pl.ds(LAT, n)]
+    wind = part_small.at[pl.ds(0, 2 * SUB)]
+    tabs = part_small.at[pl.ds(2 * SUB, SUB)]
     me = lax.axis_index("group")
     sec = lax.axis_index("sector")
     east, west = lax.rem(sec + 1, ns), lax.rem(sec + ns - 1, ns)
@@ -54,9 +54,6 @@
     for g in range(groups):
         load(g).start()
 
-    for j in range(LAT):
-        icos[j] = np.float32(1.0 / math.cos((j + 0.5 - LAT / 2) * (math.pi / 2160.0)))
-
     barrier = pltpu.get_barrier_semaphore()
 
     @pl.loop(1, n)
@@ -73,11 +70,80 @@
     def _(t):
         for i in range(SUB):
             j = t * SUB + i
-            mb[j] = jnp.broadcast_to(lm[pl.ds(j, 1), :], (SUB, LANES))
+            mb[j] = jnp.broadcast_to(lm[pl.ds(j, 1), :].astype(F32), (SUB, LANES))
+
+    sets = [list(range(EARLY)), list(range(EARLY, groups))]
+    for g in range(EARLY):
+        load(g).wait()
+
+    half = LAT // 2
+    fourth = half // 2
+    fold = SLOT * (EARLY + 1)
+
+    def window(members, j):
+        packed = pltpu.roll(mb[j], EDGE + SLOT * len(members), axis=1)
+        for i, g in enumerate(members):
+            tile = x[pl.ds(g * SUB * LAT + j, SUB, stride=LAT), :]
+            tile = pltpu.roll(tile, EDGE + SLOT * i, axis=1)
+            packed = jnp.where((lane >= SLOT * i) & (lane < SLOT * (i + 1)), tile, packed)
+        return packed
+
+    def pair(which, j):
+        low, high = window(sets[which], j), window(sets[which], j + half)
+        own[which * LAT + j] = low
+        own[which * LAT + j + half] = high
+        return (jnp.where(first, low, pltpu.roll(high, EDGE, axis=1)),
+                jnp.where(first, pltpu.roll(high, LANES - EDGE, axis=1), low))
+
+    def folded(a, b):
+        return jnp.where(lane < fold, a, pltpu.roll(b, fold, axis=1))
+
+    @pl.loop(0, fourth // 4)
+    def _(t):
+        for i in range(4):
+            j = t * 4 + i
+            ea, wa = pair(0, j)
+            eb, wb = pair(0, j + fourth)
+            te[j] = folded(ea, eb)
+            tw[j] = folded(wa, wb)
+
+    pl.semaphore_wait(barrier, n + 1)
+    starts = [0, fourth, fourth + half // 2, fourth + half]
+
+    def halo(src, dst, k, c, side):
+        rows = pl.ds(starts[c], starts[c + 1] - starts[c])
+        return pltpu.make_async_remote_copy(
+            src_ref=src.at[rows], dst_ref=dst.at[rows], send_sem=halo_send.at[k * PARTS + c],
+            recv_sem=halo_recv.at[k * PARTS + c], device_id={"sector": side}, device_id_type=MESH)
+
+    def to_east(c):
+        return halo(te, ter, 0, c, east)
+
+    def to_west(c):
+        return halo(tw, twr, 1, c, west)
+
+    to_east(0).start()
+    to_west(0).start()
+
+    for g in range(EARLY, groups):
+        load(g).wait()
+
+    @pl.loop(0, half // 4)
+    def _(t):
+        for i in range(4):
+            j = t * 4 + i
+            te[fourth + j], tw[fourth + j] = pair(1, j)
+
+    for c in (1, 2):
+        to_east(c).start()
+        to_west(c).start()
+
+    for j in range(LAT):
+        icos[j] = np.float32(1.0 / math.cos((j + 0.5 - LAT / 2) * (math.pi / 2160.0)))
 
     @pl.loop(0, total // LANES)
     def _(t):
-        row = asg[pl.ds(t, 1), :]
+        row = asg[pl.ds(t, 1), :].astype(F32)
         kcol[pl.ds(pl.multiple_of(t * LANES, LANES), LANES), :] = jnp.broadcast_to(row, (LANES, LANES)).T
 
     def parts(kind):
@@ -86,7 +152,8 @@
 
     lanef = lane.astype(F32)
 
-    tables = [jnp.broadcast_to(tabs[k:k + 1, :], (SUB, LANES)) for k in range(4)]
+    shared = jnp.broadcast_to(tabs[0:1, :], (SUB, LANES))
+    tables = [shared] * 4
     for wave in (math.cos, math.sin):
         values = jnp.zeros((SUB, LANES), F32)
         for d in range(DIRS):
@@ -94,10 +161,9 @@
         tables.append(values)
 
     def look(k, index):
-        hit = jnp.where(lanef == index, tables[k], 0.0)
+        hit = jnp.where(lanef == index + float(FREQ * k) if k < 4 else lanef == index, tables[k], 0.0)
         return jnp.broadcast_to(jnp.sum(hit, axis=1, keepdims=True), (SUB, LANES))
 
-    sets = [list(range(EARLY)), list(range(EARLY, groups))]
     strips = [[jnp.zeros((SUB, LANES), F32)] * 5 for _ in sets]
     for g in range(groups):
         which = 0 if g < EARLY else 1
@@ -115,68 +181,6 @@
         for k in range(5):
             spar[which * 5 + k] = strips[which][k]
 
-    for g in range(groups):
-        load(g).wait()
-
-    half = LAT // 2
-    fourth = half // 2
-    fold = SLOT * (EARLY + 1)
-
-    def window(members, j):
-        packed = pltpu.roll(mb[j], EDGE + SLOT * len(members), axis=1)
-        for i, g in enumerate(members):
-            tile = x[pl.ds(g * SUB * LAT + j, SUB, stride=LAT), :]
-            tile = pltpu.roll(tile, EDGE + SLOT * i, axis=1)
-            packed = jnp.where((lane >= SLOT * i) & (lane < SLOT * (i + 1)), tile, packed)
-        return packed
-
-    def pair(which, j):
-        low, high = window(sets[which], j), window(sets[which], j + half)
-        own[which * LAT + j] = low
-        own[which * LAT + j + half] = high
-        return (jnp.where(first, low, pltpu.roll(high, EDGE, axis=1)),
-                jnp.where(first, pltpu.roll(high, LANES - EDGE, axis=1), low))
-
-    def folded(a, b):
-        return jnp.where(lane < fold, a, pltpu.roll(b, fold, axis=1))
-
-    @pl.loop(0, fourth // 4)
-    def _(t):
-        for i in range(4):
-            j = t * 4 + i
-            ea, wa = pair(0, j)
-            eb, wb = pair(0, j + fourth)
-            te[j] = folded(ea, eb)
-            tw[j] = folded(wa, wb)
-
-    pl.semaphore_wait(barrier, n + 1)
-    starts = [0, fourth, fourth + half // 2, fourth + half]
-
-    def halo(src, dst, k, c, side):
-        rows = pl.ds(starts[c], starts[c + 1] - starts[c])
-        return pltpu.make_async_remote_copy(
-            src_ref=src.at[rows], dst_ref=dst.at[rows], send_sem=halo_send.at[k * PARTS + c],
-            recv_sem=halo_recv.at[k * PARTS + c], device_id={"sector": side}, device_id_type=MESH)
-
-    def to_east(c):
-        return halo(te, ter, 0, c, east)
-
-    def to_west(c):
-        return halo(tw, twr, 1, c, west)
-
-    to_east(0).start()
-    to_west(0).start()
-
-    @pl.loop(0, half // 4)
-    def _(t):
-        for i in range(4):
-            j = t * 4 + i
-            te[fourth + j], tw[fourth + j] = pair(1, j)
-
-    for c in (1, 2):
-        to_east(c).start()
-        to_west(c).start()
-
     def sweep(read, write, mask, coefs):
         rate, keep, north, sx, sy = coefs
 
@@ -357,12 +361,12 @@
     def one_hot(hit):
         return hit.astype(F32).astype(BF16)
 
-    share = tabs[0:SUB, :] * (1.0 / total)
+    share = shared * (1.0 / total)
     high = share.astype(BF16).astype(F32)
     both = jnp.concatenate([high, share - high], axis=0).astype(BF16)
-    picked = jnp.dot(both, one_hot(jnp.broadcast_to(freqq[0:1], (LANES, total)) == rowid), preferred_element_type=F32)
-    w16[...] = jnp.concatenate([jnp.broadcast_to(picked[3:4], (SUB, total)),
-                                jnp.broadcast_to(picked[SUB + 3:SUB + 4], (SUB, total))], axis=0).astype(BF16)
+    picked = jnp.dot(both, one_hot(jnp.broadcast_to(freqq[0:1], (LANES, total)) + 3.0 * FREQ == rowid), preferred_element_type=F32)
+    w16[...] = jnp.concatenate([jnp.broadcast_to(picked[0:1], (SUB, total)),
+                                jnp.broadcast_to(picked[SUB:SUB + 1], (SUB, total))], axis=0).astype(BF16)
 
     spx[...] = jnp.zeros_like(spx)
     spx[:, 0:DIRS] = sp[...]
@@ -534,6 +538,14 @@
     def _(c):
         m = lax.rem(base + 4 - turn(c), 4)
 
+        @pl.when(c == 3)
+        def _():
+            @pl.loop(1, n)
+            def _(k):
+                for h in range(HALVES):
+                    back(h, lax.rem(me + k, n)).wait_send()
+
+
         @pl.loop(0, quarter)
         def _(i):
             q = m * quarter + i
@@ -550,11 +562,6 @@
                     back_mine(h).wait()
 
             relayout(q)
-
-    @pl.loop(1, n)
-    def _(k):
-        for h in range(HALVES):
-            back(h, lax.rem(me + k, n)).wait_send()
 
     @pl.loop(0, n)
     def _(q):
@@ -566,19 +573,16 @@
     total = assignment.shape[0]
     groups = comps // SUB
     block = LAT // n
-    small = jnp.concatenate((
-        land_mask.astype(F32),
-        wind_field.reshape(2 * block, LANES),
-        jnp.pad(jnp.stack((courant, growth, whitecap, weights)), ((0, SUB - 4), (0, LANES - FREQ))),
-        jnp.pad(assignment.astype(F32).reshape(total // LANES, LANES), ((0, n - total // LANES), (0, 0))),
-    ))
+    whole_small = jnp.concatenate((land_mask, jnp.pad(assignment.reshape(total // LANES, LANES), ((0, n - total // LANES), (0, 0)))))
+    part_small = jnp.concatenate((wind_field.reshape(-1), courant, growth, whitecap, weights, jnp.zeros(((SUB - 1) * LANES,), F32)))
+    part_small = part_small.reshape(3 * SUB, LANES)
     vmem = pl.BlockSpec(memory_space=pltpu.VMEM)
     tiles = lambda count: pltpu.VMEM((count, SUB, LANES), F32)
     dma = pltpu.SemaphoreType.DMA
     call = pl.pallas_call(
         functools.partial(kernel, n, ns, comps),
         out_shape=jax.ShapeDtypeStruct((comps, LAT, LANES), F32),
-        in_specs=[pl.BlockSpec(memory_space=pl.ANY)] + [vmem] * 2,
+        in_specs=[pl.BlockSpec(memory_space=pl.ANY)] + [vmem] * 3,
         out_specs=pl.BlockSpec(memory_space=pl.ANY),
         scratch_shapes=[
             pltpu.VMEM((comps * LAT, LANES), F32),
@@ -605,7 +609,7 @@
         ],
         compiler_params=pltpu.CompilerParams(collective_id=0, has_side_effects=True, vmem_limit_bytes=48 << 20),
     )
-    return call(spectrum.reshape(comps * LAT, LANES), small, spread.transpose(1, 0, 2).reshape(FREQ * DIRS, DIRS))
+    return call(spectrum.reshape(comps * LAT, LANES), whole_small, part_small, spread.transpose(1, 0, 2).reshape(FREQ * DIRS, DIRS))
 
 
 def solution(mesh):

time: 136 us -> 134 us (0.985)
  other arithmetic: 2.97 us -> 0.86 us
where the time goes in v3:
time: 134 us
  Pallas kernels  129 us (96%)
  local copies, waits for them, and re-layouts  4.05 us (3%)
    pallas_call x1, Pallas kernels, local(): call(spectrum.reshape(comps * LAT, LANES), whole_small, part_small, sprea...  129 us
    unnamed x3, local copies, waits for them, and re-layouts  3.25 us

profile of v3, /device:TPU:1, one launch (start us, length us, event | category | flops | bytes accessed | tf_op | source)
XLA Modules:
  0.0 133.8 jit_solution(16087673546091939901)
XLA Ops:
  0.0 0.8 concatenate.7
  0.8 0.9 pad_add_fusion.whole_small
  1.7 0.0 copy-start
  1.7 1.1 copy-done
  2.7 128.9 %shard_map.91 = f32[72,128,128]{2,1,0:T(8,128)S(1)} custom-call(f32[9216,128]{1,0:T(8,128)} %bitcast.9, s32[144,128]{1,0:T(8,128)S(1)} %pad_add_fusion.whole_small, f32[24,128]{1,0:T(8,128)S(1)} %bitcast.8, f32[1152,36]{1,0:T(8,128)S(1)} %bitcast.7), custom_call_target="tpu_custom_call" | custom-call | tf_op jit(solution)/shard_map/pallas_call | solution.py:612
  131.6 2.2 %copy.11 = f32[72,128,128]{2,1,0:T(8,128)} copy(f32[72,128,128]{2,1,0:T(8,128)S(1)} %shard_map.91) | data formatting | bytes 9437184
  (1 shorter events, 0.0 us)
Async XLA Ops:
  1.7 1.1 copy-start

commit v4 on v3

--- a/solution.py
+++ b/solution.py
@@ -21,7 +21,7 @@
 EARLY = 2
 HALVES = 2
 PARTS = 3
-DEEP = 64
+DEEP = 128
 F32 = jnp.float32
 BF16 = jnp.bfloat16
 

time: 134 us -> 134 us (level)
  no operation moved by 1% of the time
where the time goes in v4:
time: 134 us
  Pallas kernels  129 us (96%)
  local copies, waits for them, and re-layouts  4.05 us (3%)
    pallas_call x1, Pallas kernels, local(): call(spectrum.reshape(comps * LAT, LANES), whole_small, part_small, sprea...  129 us
    unnamed x3, local copies, waits for them, and re-layouts  3.25 us

profile of v4, /device:TPU:1, one launch (start us, length us, event | category | flops | bytes accessed | tf_op | source)
XLA Modules:
  0.0 133.8 jit_solution(16087673546091939901)
XLA Ops:
  0.0 0.8 concatenate.7
  0.8 0.9 pad_add_fusion.whole_small
  1.7 0.0 copy-start
  1.7 1.1 copy-done
  2.7 128.9 %shard_map.91 = f32[72,128,128]{2,1,0:T(8,128)S(1)} custom-call(f32[9216,128]{1,0:T(8,128)} %bitcast.9, s32[144,128]{1,0:T(8,128)S(1)} %pad_add_fusion.whole_small, f32[24,128]{1,0:T(8,128)S(1)} %bitcast.8, f32[1152,36]{1,0:T(8,128)S(1)} %bitcast.7), custom_call_target="tpu_custom_call" | custom-call | tf_op jit(solution)/shard_map/pallas_call | solution.py:612
  131.6 2.2 %copy.11 = f32[72,128,128]{2,1,0:T(8,128)} copy(f32[72,128,128]{2,1,0:T(8,128)S(1)} %shard_map.91) | data formatting | bytes 9437184
  (1 shorter events, 0.0 us)
Async XLA Ops:
  1.7 1.1 copy-start
